TPU v7x, 32 devices: a whole 2x2x4 slice. The times are simulated.
32 devices in a mesh: ma: 16 (over z, y, core), freq: 2 (over x).
Axes of the slice: x: 2, y: 2, z: 4, core: 2. Of those that a mesh axis runs over, the one named last changes fastest.
Arguments:
- right_side: float32 [128, 8, 2, 512], P('ma', 'freq'), may hold values from -60 to 60
- start_field: float32 [128, 8, 2, 512], P('ma', 'freq'), may hold values from -6 to 6
- beam: float32 [128, 8, 2, 16, 512], P('ma', 'freq'), may hold values from -0.75 to 0.75
- noise: float32 [128, 8, 16], P('ma', 'freq'), may hold values from 0.3 to 3
- inv_power: float32 [512], replicated, may hold values from 0.5 to 2
- smooth: float32 [512], replicated, may hold values from 0.5 to 4
Outputs:
- solution_field: float32 [128, 8, 2, 512], P('ma', 'freq')
- residual: float32 [128, 8, 2, 512], P('ma', 'freq')
All inputs are finite; a program needn't handle non-finite values.
Results may differ from a plain program's by a relative error of at most 0.0003.
Values sent between devices are 32-bit elements; how exact they have to be, the bound alone decides.
A program may use at most 64 MiB of HBM per device.

v0:
```python
import jax
import jax.numpy as jnp
from jax import lax
from jax.sharding import PartitionSpec as P

ITERS = 2


def extended(array, sides, width):
    for axis, dim in sides:
        size, length = (lax.axis_size(axis), array.shape[dim])
        up = [(i, (i + 1) % size) for i in range(size - 1)]
        down = [(j, i) for i, j in up]
        last = lax.slice_in_dim(array, length - width, length, axis=dim)
        leading = lax.slice_in_dim(array, 0, width, axis=dim)
        before = lax.ppermute(last, axis, up)
        after = lax.ppermute(leading, axis, down)
        array = jnp.concatenate([before, array, after], axis=dim)
    return array


def beam_image(field, beam, noise):
    projected = jnp.einsum("mfakl,mfbl->mfabk", beam, field, precision=lax.Precision.HIGHEST)
    real_part = projected[:, :, 0, 0] + projected[:, :, 1, 1]
    imaginary = projected[:, :, 0, 1] - projected[:, :, 1, 0]
    weighted = jnp.stack([real_part, imaginary], axis=2) * noise[:, :, None, :]
    back = jnp.einsum("mfakl,mfbk->mfabl", beam, weighted, precision=lax.Precision.HIGHEST)
    return jnp.stack(
        [back[:, :, 0, 0] - back[:, :, 1, 1], back[:, :, 0, 1] + back[:, :, 1, 0]], axis=2
    )


def prior_term(padded, field, first, total, smooth):
    channel = first + jnp.arange(field.shape[1], dtype=jnp.int32)
    weight = (channel > 0).astype(jnp.float32) + (channel < total - 1).astype(jnp.float32)
    return smooth * (weight[None, :, None, None] * field - padded[:, :-2] - padded[:, 2:])


def two_products(vector, applied):
    return lax.psum((jnp.sum(vector * vector), jnp.sum(vector * applied)), ("ma", "freq"))


def shards(right_side, start_field, beam, noise, inv_power, smooth):
    first = lax.axis_index("freq") * right_side.shape[1]
    total = right_side.shape[1] * lax.axis_size("freq")

    def padded_of(field):
        return extended(field, (("freq", 1),), 1)

    def operate(field):
        prior = prior_term(padded_of(field), field, first, total, smooth)
        return beam_image(field, beam, noise) + inv_power * field + prior

    solution = start_field
    resid_now = right_side - operate(start_field)
    applied = operate(resid_now)
    norm_now, curve_now = two_products(resid_now, applied)
    step_size = norm_now / curve_now
    direction = resid_now
    along = applied
    for turn in range(ITERS):
        solution = solution + step_size * direction
        resid_now = resid_now - step_size * along
        if turn + 1 < ITERS:
            applied = operate(resid_now)
            norm_next, curve_now = two_products(resid_now, applied)
            growth = norm_next / norm_now
            step_size = norm_next / (curve_now - growth * norm_next / step_size)
            direction = resid_now + growth * direction
            along = applied + growth * along
            norm_now = norm_next
    return (solution, resid_now)


def solution(mesh):
    in_specs = (
        P("ma", "freq", None, None),
        P("ma", "freq", None, None),
        P("ma", "freq", None, None, None),
        P("ma", "freq", None),
        P(),
        P(),
    )
    out_specs = (P("ma", "freq", None, None), P("ma", "freq", None, None))
    return jax.shard_map(shards, mesh=mesh, in_specs=in_specs, out_specs=out_specs, check_vma=False)
```

profile of v0, /device:TPU:0, one launch (start us, length us, event | category | flops | bytes accessed | tf_op | source)
XLA Modules:
  0.0 144.0 jit_solution(10948142598104500641)
XLA Ops:
  0.6 0.0 copy-start
  0.7 0.9 fusion.42
  1.6 4.9 %collective-permute-start = (f32[8,1,2,512]{3,2,1,0:T(2,128)S(1)}, f32[8,1,2,512]{3,2,1,0:T(2,128)S(1)}, u32[]{:S(2)}, u32[]{:S(2)}) collective-permute-start(f32[8,1,2,512]{3,2,1,0:T(2,128)S(1)} %get-tuple-element.22), channel_id=1, source_target_pairs={{0,1},{2,3},{4,5},{6,7},{8,9},{10,11},{12,13},{14,15},{16,17},{18,... | collective-permute-start | bytes 98312 | tf_op jit(solution)/shard_map/ppermute | solution.py:16
  6.5 1.3 collective-permute-start.1
  7.8 8.3 %convolution_bitcast_fusion.1 = f32[8,4,2,2,16]{4,3,2,1,0:T(2,128)S(1)} fusion(f32[8,4,2,16,512]{4,3,2,1,0:T(8,128)S(1)} %copy-done, f32[8,4,2,512]{3,2,1,0:T(2,128)} %param.7), kind=kOutput, calls=%fused_computation.1 | convolution fusion | flops 12582912 | bytes 2236416 | tf_op jit(solution)/shard_map/mfakl,mfbl->mfabk/dot_general | solution.py:23
  16.1 0.0 copy-start.4
  16.1 0.0 copy-start.5
  16.2 1.1 convolution_bitcast_fusion
  17.3 0.1 fusion.22
  17.4 0.1 fusion.24
  17.6 0.3 fusion.11
  17.9 7.4 %fusion.15 = f32[8,4,2,2,16]{4,2,3,1,0:T(2,128)S(1)} fusion(f32[8,4,2,16,512]{4,3,2,1,0:T(8,128)S(1)} %copy-done, f32[8,4,2,512]{3,2,1,0:T(2,128)S(1)} %fusion.11), kind=kOutput, calls=%fused_computation.28 | convolution fusion | flops 12582912 | bytes 2236416 | tf_op jit(solution)/shard_map/mfakl,mfbl->mfabk/dot_general | solution.py:23
  25.4 1.3 fusion.30
  26.7 0.1 copy.46
  26.9 4.5 %collective-permute-start.2 = (f32[8,1,2,512]{3,2,1,0:T(2,128)S(1)}, f32[8,1,2,512]{3,2,1,0:T(2,128)S(1)}, u32[]{:S(2)}, u32[]{:S(2)}) collective-permute-start(f32[8,1,2,512]{3,2,1,0:T(2,128)S(1)} %get-tuple-element.20), channel_id=1, source_target_pairs={{0,1},{2,3},{4,5},{6,7},{8,9},{10,11},{12,13},{14,15},{16,17},{18,... | collective-permute-start | bytes 98312 | tf_op jit(solution)/shard_map/ppermute | solution.py:16
  31.4 1.3 collective-permute-start.3
  32.7 0.1 fusion.21
  32.9 0.1 collective-permute-done.2
  33.0 4.2 %collective-permute-done.3 = f32[8,1,2,512]{3,2,1,0:T(2,128)S(1)} collective-permute-done((f32[8,1,2,512]{3,2,1,0:T(2,128)S(1)}, f32[8,1,2,512]{3,2,1,0:T(2,128)S(1)}, u32[]{:S(2)}, u32[]{:S(2)}) %collective-permute-start.3) | collective-permute-done | bytes 32800 | tf_op jit(solution)/shard_map/ppermute | solution.py:17
  37.2 1.1 multiply_reduce_fusion.2
  38.3 39.8 %all-reduce.1 = (f32[]{:T(128)}, f32[]{:T(128)}) all-reduce(f32[]{:T(128)} %get-tuple-element.5, f32[]{:T(128)} %get-tuple-element.4), channel_id=1, replica_groups=mesh['ma'=16,'freq'=2] {'ma','freq'}, use_global_device_ids=true, to_apply=%region_1.0 | all-reduce | flops 2 | bytes 16 | tf_op jit(solution)/shard_map/psum | solution.py:40
  79.4 7.4 %fusion.13 = f32[8,4,2,2,16]{4,2,3,1,0:T(2,128)S(1)} fusion(f32[8,4,2,16,512]{4,3,2,1,0:T(8,128)S(1)} %copy-done, f32[8,4,2,512]{3,2,1,0:T(2,128)S(1)} %bitcast.90), kind=kOutput, calls=%fused_computation.26 | convolution fusion | flops 12582912 | bytes 2236416 | tf_op jit(solution)/shard_map/mfakl,mfbl->mfabk/dot_general | solution.py:23
  86.9 1.1 fusion.28
  88.0 0.1 copy.45
  88.2 4.2 %collective-permute-start.4 = (f32[8,1,2,512]{3,2,1,0:T(2,128)S(1)}, f32[8,1,2,512]{3,2,1,0:T(2,128)S(1)}, u32[]{:S(2)}, u32[]{:S(2)}) collective-permute-start(f32[8,1,2,512]{3,2,1,0:T(2,128)S(1)} %get-tuple-element.18), channel_id=1, source_target_pairs={{0,1},{2,3},{4,5},{6,7},{8,9},{10,11},{12,13},{14,15},{16,17},{18,... | collective-permute-start | bytes 98312 | tf_op jit(solution)/shard_map/ppermute | solution.py:16
  92.4 1.3 collective-permute-start.5
  93.7 0.1 fusion.19
  93.8 0.1 collective-permute-done.4
  93.9 4.2 %collective-permute-done.5 = f32[8,1,2,512]{3,2,1,0:T(2,128)S(1)} collective-permute-done((f32[8,1,2,512]{3,2,1,0:T(2,128)S(1)}, f32[8,1,2,512]{3,2,1,0:T(2,128)S(1)}, u32[]{:S(2)}, u32[]{:S(2)}) %collective-permute-start.5) | collective-permute-done | bytes 32800 | tf_op jit(solution)/shard_map/ppermute | solution.py:17
  98.2 1.1 multiply_reduce_fusion
  99.3 39.4 %all-reduce = (f32[]{:T(128)}, f32[]{:T(128)}) all-reduce(f32[]{:T(128)} %get-tuple-element.3, f32[]{:T(128)} %get-tuple-element.2), channel_id=1, replica_groups=mesh['ma'=16,'freq'=2] {'ma','freq'}, use_global_device_ids=true, to_apply=%region_5.0 | all-reduce | flops 2 | bytes 16 | tf_op jit(solution)/shard_map/psum | solution.py:40
  143.3 0.8 multiply_subtract_fusion
  (24 shorter events, 0.2 us)
Async XLA Ops:
  0.6 7.1 %copy-start = (f32[8,4,2,16,512]{4,3,2,1,0:T(8,128)S(1)}, f32[8,4,2,16,512]{4,3,2,1,0:T(8,128)}, u32[]{:S(2)}) copy-start(f32[8,4,2,16,512]{4,3,2,1,0:T(8,128)} %param.8) | copy-start | bytes 6291460
  0.6 15.5 %copy-start.2 = (f32[8,4,16]{2,1,0:T(4,128)S(1)}, f32[8,4,16]{2,1,0:T(4,128)}, u32[]{:S(2)}) copy-start(f32[8,4,16]{2,1,0:T(4,128)} %param.9) | copy-start | bytes 6148
  1.6 16.0 %collective-permute-start = (f32[8,1,2,512]{3,2,1,0:T(2,128)S(1)}, f32[8,1,2,512]{3,2,1,0:T(2,128)S(1)}, u32[]{:S(2)}, u32[]{:S(2)}) collective-permute-start(f32[8,1,2,512]{3,2,1,0:T(2,128)S(1)} %get-tuple-element.22), channel_id=1, source_target_pairs={{0,1},{2,3},{4,5},{6,7},{8,9},{10,11},{12,13},{14,15},{16,17},{18,... | collective-permute-start | bytes 98312 | tf_op jit(solution)/shard_map/ppermute | solution.py:16
  6.5 11.1 %collective-permute-start.1 = (f32[8,1,2,512]{3,2,1,0:T(2,128)S(1)}, f32[8,1,2,512]{3,2,1,0:T(2,128)S(1)}, u32[]{:S(2)}, u32[]{:S(2)}) collective-permute-start(f32[8,1,2,512]{3,2,1,0:T(2,128)S(1)} %get-tuple-element.23), channel_id=1, source_target_pairs={{1,0},{3,2},{5,4},{7,6},{9,8},{11,10},{13,12},{15,14},{17,16},{19,... | collective-permute-start | bytes 98312 | tf_op jit(solution)/shard_map/ppermute | solution.py:17
  16.1 1.5 %copy-start.1 = (f32[8,4,2,512]{3,2,1,0:T(2,128)S(1)}, f32[8,4,2,512]{3,2,1,0:T(2,128)}, u32[]{:S(2)}) copy-start(f32[8,4,2,512]{3,2,1,0:T(2,128)} %param.7) | copy-start | bytes 393220
  16.1 1.5 %copy-start.3 = (f32[8,4,2,512]{3,2,1,0:T(2,128)S(1)}, f32[8,4,2,512]{3,2,1,0:T(2,128)}, u32[]{:S(2)}) copy-start(f32[8,4,2,512]{3,2,1,0:T(2,128)} %param.6) | copy-start | bytes 393220
  16.1 1.6 %copy-start.4 = (f32[512]{0:T(512)S(1)}, f32[512]{0:T(512)}, u32[]{:S(2)}) copy-start(f32[512]{0:T(512)} %param.11) | copy-start | bytes 6148
  16.1 1.5 %copy-start.5 = (f32[512]{0:T(512)S(1)}, f32[512]{0:T(512)}, u32[]{:S(2)}) copy-start(f32[512]{0:T(512)} %param.10) | copy-start | bytes 6148
  26.9 6.1 %collective-permute-start.2 = (f32[8,1,2,512]{3,2,1,0:T(2,128)S(1)}, f32[8,1,2,512]{3,2,1,0:T(2,128)S(1)}, u32[]{:S(2)}, u32[]{:S(2)}) collective-permute-start(f32[8,1,2,512]{3,2,1,0:T(2,128)S(1)} %get-tuple-element.20), channel_id=1, source_target_pairs={{0,1},{2,3},{4,5},{6,7},{8,9},{10,11},{12,13},{14,15},{16,17},{18,... | collective-permute-start | bytes 98312 | tf_op jit(solution)/shard_map/ppermute | solution.py:16
  31.4 5.8 %collective-permute-start.3 = (f32[8,1,2,512]{3,2,1,0:T(2,128)S(1)}, f32[8,1,2,512]{3,2,1,0:T(2,128)S(1)}, u32[]{:S(2)}, u32[]{:S(2)}) collective-permute-start(f32[8,1,2,512]{3,2,1,0:T(2,128)S(1)} %get-tuple-element.21), channel_id=1, source_target_pairs={{1,0},{3,2},{5,4},{7,6},{9,8},{11,10},{13,12},{15,14},{17,16},{19,... | collective-permute-start | bytes 98312 | tf_op jit(solution)/shard_map/ppermute | solution.py:17
  88.2 5.8 %collective-permute-start.4 = (f32[8,1,2,512]{3,2,1,0:T(2,128)S(1)}, f32[8,1,2,512]{3,2,1,0:T(2,128)S(1)}, u32[]{:S(2)}, u32[]{:S(2)}) collective-permute-start(f32[8,1,2,512]{3,2,1,0:T(2,128)S(1)} %get-tuple-element.18), channel_id=1, source_target_pairs={{0,1},{2,3},{4,5},{6,7},{8,9},{10,11},{12,13},{14,15},{16,17},{18,... | collective-permute-start | bytes 98312 | tf_op jit(solution)/shard_map/ppermute | solution.py:16
  92.4 5.8 %collective-permute-start.5 = (f32[8,1,2,512]{3,2,1,0:T(2,128)S(1)}, f32[8,1,2,512]{3,2,1,0:T(2,128)S(1)}, u32[]{:S(2)}, u32[]{:S(2)}) collective-permute-start(f32[8,1,2,512]{3,2,1,0:T(2,128)S(1)} %get-tuple-element.19), channel_id=1, source_target_pairs={{1,0},{3,2},{5,4},{7,6},{9,8},{11,10},{13,12},{15,14},{17,16},{19,... | collective-permute-start | bytes 98312 | tf_op jit(solution)/shard_map/ppermute | solution.py:17
where the time goes:
time: 145 us; the launch traced here: 144 us
  blocking collectives  79.2 us (55%)
  matrix products  26.7 us (18%)
  starting transfers between devices  17.5 us (12%)
  waiting for transfers between devices  8.73 us (6%)
  between operations  6.85 us (5%)
  other arithmetic  3.86 us (3%)
    psum x2, blocking collectives, two_products(): lax.psum((jnp.sum(vector * vector), jnp.sum(vector * applied)), ('ma', 'f...  79.2 us
    dot_general x3, matrix products, beam_image(): jnp.einsum('mfakl,mfbl->mfabk', beam, field, precision=lax.Precision.HIGH...  23.1 us
    ppermute x3, starting transfers between devices, extended(): before = lax.ppermute(last, axis, up)  13.6 us
    ppermute x3, waiting for transfers between devices, extended(): after = lax.ppermute(leading, axis, down)  8.46 us
    ppermute x3, starting transfers between devices, extended(): after = lax.ppermute(leading, axis, down)  3.88 us
    dot_general x3, matrix products, beam_image(): jnp.einsum('mfakl,mfbk->mfabl', beam, weighted, precision=lax.Precision.H...  3.6 us
  transfers between devices with their start and end apart: 6, of which 4 were waited for; matrix products, arithmetic and copies ran while one was open for 7% of the time, Pallas kernels for 0%

commit v1 on v0

--- a/solution.py
+++ b/solution.py
@@ -37,7 +37,7 @@
 
 
 def two_products(vector, applied):
-    return lax.psum((jnp.sum(vector * vector), jnp.sum(vector * applied)), ("ma", "freq"))
+    return lax.psum(lax.psum((jnp.sum(vector * vector), jnp.sum(vector * applied)), "ma"), "freq")
 
 
 def shards(right_side, start_field, beam, noise, inv_power, smooth):

time: 145 us -> 136 us (0.938)
  blocking collectives: 79.2 us -> 73.4 us
  starting transfers between devices: 17.5 us -> 15.2 us
    psum x2 -> x4, blocking collectives: 79.2 us -> 73.4 us  [the longest x2 62.2 us: two_products(): lax.psum((jnp.sum(vector * vector), jnp.sum(vector * applied)), 'ma')]
    ppermute x3, starting transfers between devices: 13.6 us -> 11.3 us  [extended(): before = lax.ppermute(last, axis, up)]
where the time goes in v1:
time: 136 us
  blocking collectives  73.4 us (54%)
  matrix products  26.7 us (20%)
  starting transfers between devices  15.2 us (11%)
  waiting for transfers between devices  8.73 us (6%)
  between operations  6.7 us (5%)
  other arithmetic  3.87 us (3%)
    psum x2, blocking collectives, two_products(): lax.psum((jnp.sum(vector * vector), jnp.sum(vector * applied)), 'ma')  62.2 us
    dot_general x3, matrix products, beam_image(): jnp.einsum('mfakl,mfbl->mfabk', beam, field, precision=lax.Precision.HIGH...  23.1 us
    ppermute x3, starting transfers between devices, extended(): before = lax.ppermute(last, axis, up)  11.3 us
    psum x2, blocking collectives, two_products(): lax.psum(lax.psum((jnp.sum(vector * vector), jnp.sum(vector * applied)),...  11.2 us
    ppermute x3, waiting for transfers between devices, extended(): after = lax.ppermute(leading, axis, down)  8.46 us
    ppermute x3, starting transfers between devices, extended(): after = lax.ppermute(leading, axis, down)  3.88 us
    dot_general x3, matrix products, beam_image(): jnp.einsum('mfakl,mfbk->mfabl', beam, weighted, precision=lax.Precision.H...  3.6 us
  transfers between devices with their start and end apart: 6, of which 4 were waited for; matrix products, arithmetic and copies ran while one was open for 7% of the time, Pallas kernels for 0%

profile of v1, /device:TPU:0, one launch (start us, length us, event | category | flops | bytes accessed | tf_op | source)
XLA Modules:
  0.0 135.9 jit_solution(16923702182581727259)
XLA Ops:
  0.7 0.9 fusion.42
  1.6 4.9 %collective-permute-start = (f32[8,1,2,512]{3,2,1,0:T(2,128)S(1)}, f32[8,1,2,512]{3,2,1,0:T(2,128)S(1)}, u32[]{:S(2)}, u32[]{:S(2)}) collective-permute-start(f32[8,1,2,512]{3,2,1,0:T(2,128)S(1)} %get-tuple-element.26), channel_id=1, source_target_pairs={{0,1},{2,3},{4,5},{6,7},{8,9},{10,11},{12,13},{14,15},{16,17},{18,... | collective-permute-start | bytes 98312 | tf_op jit(solution)/shard_map/ppermute | solution.py:16
  6.5 1.3 collective-permute-start.1
  7.8 8.3 %convolution_bitcast_fusion.1 = f32[8,4,2,2,16]{4,3,2,1,0:T(2,128)S(1)} fusion(f32[8,4,2,16,512]{4,3,2,1,0:T(8,128)S(1)} %copy-done, f32[8,4,2,512]{3,2,1,0:T(2,128)} %param.7), kind=kOutput, calls=%fused_computation.1 | convolution fusion | flops 12582912 | bytes 2236416 | tf_op jit(solution)/shard_map/mfakl,mfbl->mfabk/dot_general | solution.py:23
  16.1 0.0 copy-start.4
  16.2 1.1 convolution_bitcast_fusion
  17.3 0.1 fusion.22
  17.4 0.1 fusion.24
  17.6 0.3 fusion.11
  17.9 7.4 %fusion.15 = f32[8,4,2,2,16]{4,2,3,1,0:T(2,128)S(1)} fusion(f32[8,4,2,16,512]{4,3,2,1,0:T(8,128)S(1)} %copy-done, f32[8,4,2,512]{3,2,1,0:T(2,128)S(1)} %fusion.11), kind=kOutput, calls=%fused_computation.28 | convolution fusion | flops 12582912 | bytes 2236416 | tf_op jit(solution)/shard_map/mfakl,mfbl->mfabk/dot_general | solution.py:23
  25.4 1.3 fusion.30
  26.7 0.1 copy.46
  26.9 4.5 %collective-permute-start.2 = (f32[8,1,2,512]{3,2,1,0:T(2,128)S(1)}, f32[8,1,2,512]{3,2,1,0:T(2,128)S(1)}, u32[]{:S(2)}, u32[]{:S(2)}) collective-permute-start(f32[8,1,2,512]{3,2,1,0:T(2,128)S(1)} %get-tuple-element.24), channel_id=1, source_target_pairs={{0,1},{2,3},{4,5},{6,7},{8,9},{10,11},{12,13},{14,15},{16,17},{18,... | collective-permute-start | bytes 98312 | tf_op jit(solution)/shard_map/ppermute | solution.py:16
  31.4 1.3 collective-permute-start.3
  32.7 0.1 fusion.21
  32.9 0.1 collective-permute-done.2
  33.0 4.2 %collective-permute-done.3 = f32[8,1,2,512]{3,2,1,0:T(2,128)S(1)} collective-permute-done((f32[8,1,2,512]{3,2,1,0:T(2,128)S(1)}, f32[8,1,2,512]{3,2,1,0:T(2,128)S(1)}, u32[]{:S(2)}, u32[]{:S(2)}) %collective-permute-start.3) | collective-permute-done | bytes 32800 | tf_op jit(solution)/shard_map/ppermute | solution.py:17
  37.2 1.1 multiply_reduce_fusion.2
  38.3 32.1 %all-reduce.1 = (f32[]{:T(128)}, f32[]{:T(128)}) all-reduce(f32[]{:T(128)} %get-tuple-element.5, f32[]{:T(128)} %get-tuple-element.4), channel_id=1, replica_groups=mesh['ma'=16,'freq'=2] {'ma'}, use_global_device_ids=true, to_apply=%region_1.0 | all-reduce | flops 2 | bytes 16 | tf_op jit(solution)/shard_map/psum | solution.py:40
  70.4 5.5 %all-reduce.3 = (f32[]{:T(128)}, f32[]{:T(128)}) all-reduce(f32[]{:T(128)} %get-tuple-element.8, f32[]{:T(128)} %get-tuple-element.9), channel_id=1, replica_groups=mesh['ma'=16,'freq'=2] {'freq'}, use_global_device_ids=true, to_apply=%region_2.0 | all-reduce | flops 2 | bytes 16 | tf_op jit(solution)/shard_map/psum | solution.py:40
  77.3 7.4 %fusion.13 = f32[8,4,2,2,16]{4,2,3,1,0:T(2,128)S(1)} fusion(f32[8,4,2,16,512]{4,3,2,1,0:T(8,128)S(1)} %copy-done, f32[8,4,2,512]{3,2,1,0:T(2,128)S(1)} %bitcast.90), kind=kOutput, calls=%fused_computation.26 | convolution fusion | flops 12582912 | bytes 2236416 | tf_op jit(solution)/shard_map/mfakl,mfbl->mfabk/dot_general | solution.py:23
  84.8 1.1 fusion.28
  85.9 0.1 copy.45
  86.1 1.9 %collective-permute-start.4 = (f32[8,1,2,512]{3,2,1,0:T(2,128)S(1)}, f32[8,1,2,512]{3,2,1,0:T(2,128)S(1)}, u32[]{:S(2)}, u32[]{:S(2)}) collective-permute-start(f32[8,1,2,512]{3,2,1,0:T(2,128)S(1)} %get-tuple-element.22), channel_id=1, source_target_pairs={{0,1},{2,3},{4,5},{6,7},{8,9},{10,11},{12,13},{14,15},{16,17},{18,... | collective-permute-start | bytes 98312 | tf_op jit(solution)/shard_map/ppermute | solution.py:16
  88.0 1.3 collective-permute-start.5
  89.3 0.1 fusion.19
  89.4 0.1 collective-permute-done.4
  89.6 4.2 %collective-permute-done.5 = f32[8,1,2,512]{3,2,1,0:T(2,128)S(1)} collective-permute-done((f32[8,1,2,512]{3,2,1,0:T(2,128)S(1)}, f32[8,1,2,512]{3,2,1,0:T(2,128)S(1)}, u32[]{:S(2)}, u32[]{:S(2)}) %collective-permute-start.5) | collective-permute-done | bytes 32800 | tf_op jit(solution)/shard_map/ppermute | solution.py:17
  93.8 1.1 multiply_reduce_fusion
  95.0 30.1 %all-reduce = (f32[]{:T(128)}, f32[]{:T(128)}) all-reduce(f32[]{:T(128)} %get-tuple-element.3, f32[]{:T(128)} %get-tuple-element.2), channel_id=1, replica_groups=mesh['ma'=16,'freq'=2] {'ma'}, use_global_device_ids=true, to_apply=%region_7.0 | all-reduce | flops 2 | bytes 16 | tf_op jit(solution)/shard_map/psum | solution.py:40
  125.1 5.6 %all-reduce.2 = (f32[]{:T(128)}, f32[]{:T(128)}) all-reduce(f32[]{:T(128)} %get-tuple-element.6, f32[]{:T(128)} %get-tuple-element.7), channel_id=1, replica_groups=mesh['ma'=16,'freq'=2] {'freq'}, use_global_device_ids=true, to_apply=%region_8.0 | all-reduce | flops 2 | bytes 16 | tf_op jit(solution)/shard_map/psum | solution.py:40
  135.1 0.8 multiply_subtract_fusion
  (26 shorter events, 0.2 us)
Async XLA Ops:
  0.6 7.1 %copy-start = (f32[8,4,2,16,512]{4,3,2,1,0:T(8,128)S(1)}, f32[8,4,2,16,512]{4,3,2,1,0:T(8,128)}, u32[]{:S(2)}) copy-start(f32[8,4,2,16,512]{4,3,2,1,0:T(8,128)} %param.8) | copy-start | bytes 6291460
  0.6 15.5 %copy-start.2 = (f32[8,4,16]{2,1,0:T(4,128)S(1)}, f32[8,4,16]{2,1,0:T(4,128)}, u32[]{:S(2)}) copy-start(f32[8,4,16]{2,1,0:T(4,128)} %param.9) | copy-start | bytes 6148
  1.6 16.0 %collective-permute-start = (f32[8,1,2,512]{3,2,1,0:T(2,128)S(1)}, f32[8,1,2,512]{3,2,1,0:T(2,128)S(1)}, u32[]{:S(2)}, u32[]{:S(2)}) collective-permute-start(f32[8,1,2,512]{3,2,1,0:T(2,128)S(1)} %get-tuple-element.26), channel_id=1, source_target_pairs={{0,1},{2,3},{4,5},{6,7},{8,9},{10,11},{12,13},{14,15},{16,17},{18,... | collective-permute-start | bytes 98312 | tf_op jit(solution)/shard_map/ppermute | solution.py:16
  6.5 11.1 %collective-permute-start.1 = (f32[8,1,2,512]{3,2,1,0:T(2,128)S(1)}, f32[8,1,2,512]{3,2,1,0:T(2,128)S(1)}, u32[]{:S(2)}, u32[]{:S(2)}) collective-permute-start(f32[8,1,2,512]{3,2,1,0:T(2,128)S(1)} %get-tuple-element.27), channel_id=1, source_target_pairs={{1,0},{3,2},{5,4},{7,6},{9,8},{11,10},{13,12},{15,14},{17,16},{19,... | collective-permute-start | bytes 98312 | tf_op jit(solution)/shard_map/ppermute | solution.py:17
  16.1 1.5 %copy-start.1 = (f32[8,4,2,512]{3,2,1,0:T(2,128)S(1)}, f32[8,4,2,512]{3,2,1,0:T(2,128)}, u32[]{:S(2)}) copy-start(f32[8,4,2,512]{3,2,1,0:T(2,128)} %param.7) | copy-start | bytes 393220
  16.1 1.5 %copy-start.3 = (f32[8,4,2,512]{3,2,1,0:T(2,128)S(1)}, f32[8,4,2,512]{3,2,1,0:T(2,128)}, u32[]{:S(2)}) copy-start(f32[8,4,2,512]{3,2,1,0:T(2,128)} %param.6) | copy-start | bytes 393220
  16.1 1.6 %copy-start.4 = (f32[512]{0:T(512)S(1)}, f32[512]{0:T(512)}, u32[]{:S(2)}) copy-start(f32[512]{0:T(512)} %param.11) | copy-start | bytes 6148
  16.1 1.5 %copy-start.5 = (f32[512]{0:T(512)S(1)}, f32[512]{0:T(512)}, u32[]{:S(2)}) copy-start(f32[512]{0:T(512)} %param.10) | copy-start | bytes 6148
  26.9 6.1 %collective-permute-start.2 = (f32[8,1,2,512]{3,2,1,0:T(2,128)S(1)}, f32[8,1,2,512]{3,2,1,0:T(2,128)S(1)}, u32[]{:S(2)}, u32[]{:S(2)}) collective-permute-start(f32[8,1,2,512]{3,2,1,0:T(2,128)S(1)} %get-tuple-element.24), channel_id=1, source_target_pairs={{0,1},{2,3},{4,5},{6,7},{8,9},{10,11},{12,13},{14,15},{16,17},{18,... | collective-permute-start | bytes 98312 | tf_op jit(solution)/shard_map/ppermute | solution.py:16
  31.4 5.8 %collective-permute-start.3 = (f32[8,1,2,512]{3,2,1,0:T(2,128)S(1)}, f32[8,1,2,512]{3,2,1,0:T(2,128)S(1)}, u32[]{:S(2)}, u32[]{:S(2)}) collective-permute-start(f32[8,1,2,512]{3,2,1,0:T(2,128)S(1)} %get-tuple-element.25), channel_id=1, source_target_pairs={{1,0},{3,2},{5,4},{7,6},{9,8},{11,10},{13,12},{15,14},{17,16},{19,... | collective-permute-start | bytes 98312 | tf_op jit(solution)/shard_map/ppermute | solution.py:17
  86.1 3.5 %collective-permute-start.4 = (f32[8,1,2,512]{3,2,1,0:T(2,128)S(1)}, f32[8,1,2,512]{3,2,1,0:T(2,128)S(1)}, u32[]{:S(2)}, u32[]{:S(2)}) collective-permute-start(f32[8,1,2,512]{3,2,1,0:T(2,128)S(1)} %get-tuple-element.22), channel_id=1, source_target_pairs={{0,1},{2,3},{4,5},{6,7},{8,9},{10,11},{12,13},{14,15},{16,17},{18,... | collective-permute-start | bytes 98312 | tf_op jit(solution)/shard_map/ppermute | solution.py:16
  88.0 5.8 %collective-permute-start.5 = (f32[8,1,2,512]{3,2,1,0:T(2,128)S(1)}, f32[8,1,2,512]{3,2,1,0:T(2,128)S(1)}, u32[]{:S(2)}, u32[]{:S(2)}) collective-permute-start(f32[8,1,2,512]{3,2,1,0:T(2,128)S(1)} %get-tuple-element.23), channel_id=1, source_target_pairs={{1,0},{3,2},{5,4},{7,6},{9,8},{11,10},{13,12},{15,14},{17,16},{19,... | collective-permute-start | bytes 98312 | tf_op jit(solution)/shard_map/ppermute | solution.py:17
